TPU v7x, 128 devices: a whole 4x4x4 slice. The times are simulated.
128 devices in a mesh: tp: 4 (over z_lo, core), ep: 32 (over y, x, z_hi).
Axes of the slice: x: 4, y: 4, z: 4 (z_hi: 2, z_lo: 2; z = z_hi * 2 + z_lo), core: 2. Of those that a mesh axis runs over, the one named last changes fastest.
Arguments:
- hidden_in: bfloat16 [4096, 7168], P('ep', 'tp'), may hold values from -6 to 6
- next_ids: int32 [4096], P('ep'), may hold values from 0 to 65535, as said below
- embed_table: bfloat16 [65536, 7168], P('ep', 'tp'), may hold values from -6 to 6
- hidden_gain: float32 [7168], replicated, may hold values from 0.5 to 1.5
- embed_gain: float32 [7168], replicated, may hold values from 0.5 to 1.5
- ffn_gain: float32 [7168], P('tp'), may hold values from 0.5 to 1.5
- proj_weight: bfloat16 [2, 7168, 7168], P(None, 'ep', 'tp'), may hold values from -0.046875 to 0.046875
- routes: int32 [4096, 8], P('ep'), may hold values from 0 to 31, all different within a row; in each aligned block of 128 rows (0 to 127, 128 to 255, ...) at most 40 rows name the same one
- route_weights: float32 [4096, 8], P('ep'), may hold values from 0.05 to 0.5
- w_gate_up: bfloat16 [32, 7168, 2, 1024], P('ep', 'tp'), may hold values from -0.0625 to 0.0625
- w_down: bfloat16 [32, 1024, 7168], P('ep', None, 'tp'), may hold values from -0.1875 to 0.1875
- shared_gate_up: bfloat16 [7168, 2, 1024], P(('tp', 'ep')), may hold values from -0.0625 to 0.0625
- shared_down: bfloat16 [1024, 7168], P('ep', 'tp'), may hold values from -0.1875 to 0.1875
Outputs:
- module_out: bfloat16 [4096, 7168], P('ep', 'tp')
Inputs may be any that keep to these rules, and one draw needn't show every extreme that they name: `routes`: each row names 8 different experts. Among the 128 rows of one index of ep no expert is named by more than 40 rows, and in some of them one expert is named by exactly 40. `next_ids`: vocabulary row v lies with index v // 2048 of ep. Among the 128 tokens of one index of ep at most 8 have their next token with one such index, and in every index of ep one is reached by exactly 8.
All inputs are finite; a program needn't handle non-finite values.
Results may differ from a plain program's by a relative error of at most 0.03.
Values may be sent and summed in bfloat16 or wider, within the bound.
No kernel may reach another device: no remote copies, remote signals or barrier semaphores. Data moves between devices by JAX's collectives and lax.ppermute only.
A program may use at most 128 MiB of HBM per device.

v0:
```python
import jax
import jax.numpy as jnp
from jax import lax
from jax.experimental import pallas as pl
from jax.experimental.pallas import tpu as pltpu
from jax.sharding import Mesh
from jax.sharding import PartitionSpec as P

EP = ("ep_0", "ep_1", "ep_2")
XZ = ("ep_1", "ep_2")
TP_EP = ("tp", "ep_0", "ep_1", "ep_2")
BF = jnp.bfloat16
F32 = jnp.float32


def params(*semantics):
    return pltpu.CompilerParams(dimension_semantics=semantics)


def cost(flops, moved):
    return pl.CostEstimate(flops=int(flops), bytes_accessed=int(moved), transcendentals=0)


def swap(value, bit):
    return lax.ppermute(value, "tp", [(i, i ^ bit) for i in range(4)])


def shift(value, axis, by):
    size = lax.axis_size(axis)
    return lax.ppermute(value, axis, [(i, (i + by) % size) for i in range(size)])


def after(value, *earlier):
    return lax.optimization_barrier((value, *earlier))[0]


def together(*values):
    return lax.optimization_barrier(values)


def stacked(value, axis, moved):
    me = lax.axis_index(axis)
    whole = jnp.zeros((4, *value.shape), value.dtype)
    for by, piece in moved.items():
        whole = lax.dynamic_update_index_in_dim(whole, piece, (me - by) % 4, 0)
    return lax.dynamic_update_index_in_dim(whole, value, me, 0)


def padded(part):
    return -(-part // 128) * 128


def feature_blocks(rows, scale, gain, count):
    n, width = rows.shape
    part = width // count
    room = padded(part)

    def kernel(x_ref, s_ref, g_ref, o_ref):
        v = x_ref[...].astype(F32) * s_ref[...] * g_ref[...]
        o_ref[...] = jnp.zeros_like(o_ref)
        for b in range(count):
            o_ref[b, :, 0:part] = v[:, b * part : (b + 1) * part].astype(BF)

    return pl.pallas_call(
        kernel,
        out_shape=jax.ShapeDtypeStruct((count, n, room), BF),
        cost_estimate=cost(4 * n * width, 4 * n * width),
    )(rows, scale, gain)


def found_blocks(asked, table, scales, gain, planes, count):
    holders, half = asked.shape[0], asked.shape[1] // 2
    slots = holders * half
    vocab, width = table.shape
    part = width // count
    room = padded(part)
    step = 512
    each = slots // planes

    def kernel(i_ref, t_ref, s_ref, g_ref, o_ref, acc, sc):
        k = pl.program_id(0)

        @pl.when(k == 0)
        def _():
            acc[...] = jnp.zeros_like(acc)
            sc[...] = jnp.zeros_like(sc)

        ids = i_ref[...].reshape(slots, 128)[:, 0:1] - 1
        hit = ids == lax.broadcasted_iota(jnp.int32, (slots, step), 1) + k * step
        acc[...] += jnp.dot(
            jnp.where(hit, 1.0, 0.0).astype(BF), t_ref[...], preferred_element_type=F32
        )
        sc[...] += jnp.sum(jnp.where(hit, s_ref[...], 0.0), axis=1, keepdims=True)

        @pl.when(k == pl.num_programs(0) - 1)
        def _():
            v = acc[...] * sc[...] * g_ref[...]
            o_ref[...] = jnp.zeros_like(o_ref)
            for b in range(count):
                piece = v[:, b * part : (b + 1) * part].astype(BF)
                for y in range(planes):
                    o_ref[y, b, :, 0:part] = piece[y * each : (y + 1) * each]

    return pl.pallas_call(
        kernel,
        grid=(vocab // step,),
        in_specs=[
            pl.BlockSpec((holders, half, 128), lambda k: (0, 0, 0)),
            pl.BlockSpec((step, width), lambda k: (k, 0)),
            pl.BlockSpec((1, step), lambda k: (0, k)),
            pl.BlockSpec((1, width), lambda k: (0, 0)),
        ],
        out_specs=pl.BlockSpec((planes, count, each, room), lambda k: (0, 0, 0, 0)),
        out_shape=jax.ShapeDtypeStruct((planes, count, each, room), BF),
        scratch_shapes=[pltpu.VMEM((slots, width), F32), pltpu.VMEM((slots, 1), F32)],
        compiler_params=params("arbitrary"),
        cost_estimate=cost(2 * slots * vocab * width, 2 * vocab * width),
    )(asked, table, scales, gain)


def picked_blocks(first, arrived, asked, sources, tokens):
    holders, rows, room = arrived.shape
    each = rows // sources
    slots = holders * each

    def kernel(f_ref, a_ref, p_ref, o_ref):
        hit = lax.broadcasted_iota(jnp.int32, (slots, tokens), 0) == p_ref[0, 0:1, :]
        o_ref[0] = lax.dot_general(
            jnp.where(hit, 1.0, 0.0).astype(BF),
            a_ref[...].reshape(slots, room),
            (((0,), (0,)), ((), ())),
            preferred_element_type=F32,
        ).astype(BF)

    return pl.pallas_call(
        kernel,
        grid_spec=pltpu.PrefetchScalarGridSpec(
            num_scalar_prefetch=1,
            grid=(sources,),
            in_specs=[
                pl.BlockSpec((holders, each, room), lambda s, f: (0, s, 0)),
                pl.BlockSpec((1, asked.shape[1] // 2, tokens), lambda s, f: (f[0] + s, 1, 0)),
            ],
            out_specs=pl.BlockSpec((1, tokens, room), lambda s, f: (s, 0, 0)),
        ),
        out_shape=jax.ShapeDtypeStruct((sources, tokens, room), BF),
        compiler_params=params("arbitrary"),
        cost_estimate=cost(2 * sources * slots * tokens * room, 4 * holders * rows * room),
    )(first, arrived, asked)


def gained_columns(blocks, weights, gain, count):
    depth, _, width = weights.shape
    part = width // count
    step = depth // 8
    picked = blocks.shape[0]

    def kernel(at, w_ref, g_ref, o_ref):
        g = g_ref[...]
        o_ref[:, 0:part] = (w_ref[:, 0, :].astype(F32) * g).astype(BF)
        o_ref[:, part : 2 * part] = (w_ref[:, 1, :].astype(F32) * g).astype(BF)

    return pl.pallas_call(
        kernel,
        grid_spec=pltpu.PrefetchScalarGridSpec(
            num_scalar_prefetch=1,
            grid=(8, picked),
            in_specs=[
                pl.BlockSpec((step, 2, part), lambda k, b, at: (k, 0, at[b])),
                pl.BlockSpec((step, 1), lambda k, b, at: (k, 0)),
            ],
            out_specs=pl.BlockSpec((step, 2 * part), lambda k, b, at: (k, b)),
        ),
        out_shape=jax.ShapeDtypeStruct((depth, picked * 2 * part), BF),
        compiler_params=params("arbitrary", "arbitrary"),
        cost_estimate=cost(2 * depth * width, 4 * depth * width),
    )(blocks, weights, gain)


def product(rows, weights):
    return jnp.dot(rows, weights, preferred_element_type=F32)


def ranked(marks):
    rows = marks.shape[0]
    below = jnp.tril(jnp.ones((rows, rows), BF), -1)
    return jnp.dot(below, marks.astype(BF), preferred_element_type=F32).astype(jnp.int32)


def on_device(
    hidden_in,
    next_ids,
    embed_table,
    hidden_gain,
    embed_gain,
    ffn_gain,
    proj_weight,
    routes,
    route_weights,
    w_gate_up,
    w_down,
    shared_gate_up,
    shared_down,
):
    tokens, width = hidden_in.shape
    ep = lax.axis_size(EP)
    plane = lax.axis_size(XZ)
    planes = ep // plane
    vocab = embed_table.shape[0]
    model = width * 4
    t = lax.axis_index("tp")
    y = lax.axis_index("ep_0")
    x = lax.axis_index("ep_1")
    z = lax.axis_index("ep_2")
    experts = jnp.arange(ep, dtype=jnp.int32)

    id_slots = 2 * tokens // ep
    holder = next_ids // vocab
    marks = holder[:, None] == experts[None, :]
    order = jnp.sum(jnp.where(marks, ranked(marks), 0), axis=1)
    place = holder * id_slots + order
    slot_list = jnp.arange(ep * id_slots, dtype=jnp.int32)
    local_id = next_ids - holder * vocab + 1
    asked = jnp.sum(jnp.where(slot_list[:, None] == place[None, :], local_id[None, :], 0), axis=1)
    asked = jnp.broadcast_to(asked.reshape(ep, id_slots, 1), (ep, id_slots, 128))
    listed = jnp.broadcast_to(place[None, None, :], (ep, id_slots, tokens))
    asked = jnp.concatenate([asked, listed], axis=1)
    ids = lax.all_to_all(asked, EP, split_axis=0, concat_axis=0, tiled=True)

    def moved(half, gate, steps):
        own = after(proj_weight[half], gate)
        return {0: own, **{by: shift(own, "ep_0", by) for by in steps}}

    def lined(pieces):
        whole = jnp.zeros((4, padded(proj_weight.shape[1]), width), BF)
        for by, piece in pieces.items():
            whole = lax.dynamic_update_slice(whole, piece[None], (t ^ ((y - by) % 4), 0, 0))
        return whole.reshape(-1, width)

    hidden_pieces = moved(0, asked, (1, 3, 2))

    wide_hidden = after(hidden_in, asked).astype(F32)
    wide_table = after(embed_table, asked).astype(F32)
    squares = jnp.sum(wide_table * wide_table, axis=1)
    squares = jnp.concatenate([squares, jnp.sum(wide_hidden * wide_hidden, axis=1)])
    squares = squares.reshape(-1, 128)
    squares = squares + swap(squares, 1)
    squares = (squares + swap(squares, 2)).reshape(-1)
    scales = lax.rsqrt(squares / model + 1e-06)
    hidden_gain = lax.dynamic_slice(hidden_gain, (t * width,), (width,))[None, :]
    embed_gain = lax.dynamic_slice(embed_gain, (t * width,), (width,))[None, :]

    def over_tp(own):
        other = swap(own, 2)
        return [own, swap(own, 1), other, swap(other, 1)]

    blocks = feature_blocks(hidden_in, scales[vocab:, None], hidden_gain, plane)
    blocks = lax.all_to_all(blocks, XZ, split_axis=0, concat_axis=0, tiled=True)

    def side_by_side(own):
        return jnp.concatenate(over_tp(own.reshape(plane * tokens, -1)), axis=1)

    found = found_blocks(ids, embed_table, scales[None, :vocab], embed_gain, planes, plane)
    found = after(found.reshape(ep, plane * id_slots, -1), blocks)
    embed_pieces = moved(1, found, (1, 3, 2))
    gain_column = ffn_gain[:, None]

    def columns(which, gate):
        return gained_columns(
            jnp.stack(which).astype(jnp.int32), after(w_gate_up, gate), gain_column, 4
        )

    def both_of_pair(shard):
        return shard, shift(shard, "ep_2", 1)

    def of_pair(own, other, gate):
        other = after(other, gate)
        return jnp.where(z == 0, jnp.concatenate([own, other]), jnp.concatenate([other, own]))

    def of_line(row, axis):
        return stacked(row, axis, {by: shift(row, axis, by) for by in (1, 3, 2)})

    gate_up_row = both_of_pair(after(shared_gate_up, found))
    down_row = both_of_pair(after(shared_down, found))

    found = lax.all_to_all(found, EP, split_axis=0, concat_axis=0, tiled=True)
    first = (y * plane).astype(jnp.int32).reshape(1)
    embed_blocks = picked_blocks(first, found, ids, plane, tokens)
    embed_acts = side_by_side(embed_blocks)
    hidden_acts = side_by_side(blocks)
    for by in (1, 3, 2):
        hidden_pieces[by] = after(hidden_pieces[by], embed_blocks)
    start = product(hidden_acts, lined(hidden_pieces)).astype(BF)
    gate_up_row = of_pair(*gate_up_row, embed_blocks)
    down_row = of_pair(*down_row, embed_blocks)
    gate_up_row = of_line(gate_up_row, "ep_1")
    gate_up_row = gate_up_row.reshape(-1, *shared_gate_up.shape[1:])
    for by in (1, 3, 2):
        embed_pieces[by] = after(embed_pieces[by], start)
    partial = (product(embed_acts, lined(embed_pieces)) + start.astype(F32)).astype(BF)

    top = routes.shape[1]
    capacity = min(tokens, tokens * top * 5 // (4 * ep))
    routes = after(routes, partial)
    named = routes[:, :, None] == experts[None, None, :]
    hits = jnp.any(named, axis=1)
    share = jnp.sum(jnp.where(named, route_weights[:, :, None], 0.0), axis=1)
    rank = jnp.where(hits, ranked(hits), -1)
    taken = rank.T[:, None, :] == jnp.arange(capacity, dtype=jnp.int32)[None, :, None]
    send = taken.astype(BF).reshape(ep * capacity, tokens)
    combine = jnp.where(taken, share.T[:, None, :], 0.0).astype(BF)
    combine = combine.reshape(ep * capacity, tokens)

    far_columns = columns([t ^ 3, t ^ 1], partial)
    near_columns = columns([t ^ 2, t], partial)
    down_block = after(w_down, partial).reshape(4, -1, width)
    down_block = jnp.concatenate(
        [lax.dynamic_index_in_dim(down_block, t ^ q, 0, keepdims=False) for q in range(4)]
    )

    gate_up_row = after(gate_up_row, partial)
    gate_up_lines = {by: shift(gate_up_row, "ep_0", by) for by in (1, 3)}
    down_row = of_line(after(down_row, partial), "ep_0")
    sums = lax.all_to_all(
        partial.reshape(plane, tokens, width), XZ, split_axis=0, concat_axis=0, tiled=True
    )
    sums, far_columns, near_columns, down_block, send, combine = together(
        sums, far_columns, near_columns, down_block, send, combine
    )
    sums, down_row, gate_up_lines[1], gate_up_lines[3] = together(
        sums, down_row, gate_up_lines[1], gate_up_lines[3]
    )
    projected = sums.astype(F32).sum(axis=0).astype(BF)

    outgoing = jnp.dot(send, projected, preferred_element_type=F32).astype(BF)
    arrived = lax.all_to_all(
        outgoing.reshape(ep, capacity, width), EP, split_axis=0, concat_axis=0, tiled=True
    )

    def gated(pair, scale):
        hidden = pair.shape[-1] // 2
        pair = pair * scale
        return (jax.nn.silu(pair[:, :hidden]) * pair[:, hidden:]).astype(BF)

    rows = arrived.reshape(ep * capacity, width)
    gate_up_lines[2] = shift(after(gate_up_row, arrived), "ep_0", 2)
    down_row = after(down_row, arrived)
    down_lines = {by: shift(down_row, "ep_1", by) for by in (1, 3, 2)}
    far = product(rows, far_columns).astype(BF)
    far = swap(far, 1)
    near = product(rows, near_columns).astype(BF)
    half = near.shape[1] // 2

    def both(a, b, part):
        return a[:, part * half :][:, :half].astype(F32) + b[:, part * half :][:, :half].astype(F32)

    across = both(far, near, 0).astype(BF)
    wide = after(rows, across).astype(F32)
    squares = jnp.sum(wide * wide, axis=1).reshape(-1, 128)
    squares = squares + swap(squares, 1)
    squares = squares + swap(squares, 2)
    slot_scale = lax.rsqrt(squares / model + 1e-06).reshape(-1, 1)
    across = swap(across, 2)
    act = gated(both(far, near, 1) + across.astype(F32), slot_scale)
    acts = jnp.concatenate(over_tp(act), axis=1)
    acts, gate_up_lines[2] = together(acts, gate_up_lines[2])
    for by in (1, 3, 2):
        acts, down_lines[by] = together(acts, down_lines[by])
    result = product(acts, down_block).astype(BF)
    returned = lax.all_to_all(
        result.reshape(ep, capacity, width), EP, split_axis=0, concat_axis=0, tiled=True
    )

    wide = after(projected, result).astype(F32)
    squares = jnp.sum(wide * wide, axis=1).reshape(1, tokens)
    squares = squares + swap(squares, 1)
    squares = squares + swap(squares, 2)
    row_scale = lax.rsqrt(squares / model + 1e-06).reshape(tokens, 1)

    gate_up_row, down_row = after(gate_up_row, result), after(down_row, result)
    shared_columns = stacked(gate_up_row, "ep_0", gate_up_lines).reshape(width, 2, -1)
    shared_columns = jnp.concatenate(
        [(shared_columns[:, j].astype(F32) * gain_column).astype(BF) for j in range(2)], axis=1
    )
    shared_pair = product(projected, shared_columns).astype(BF).reshape(tokens, 2, 4, -1)

    def of_tp(which):
        block = lax.dynamic_index_in_dim(shared_pair, which, 2, keepdims=False)
        return block.reshape(tokens, -1).astype(F32)

    def sent(which):
        return of_tp(which).astype(BF)

    far = [swap(sent(t ^ 3), 1), swap(sent(t ^ 1), 1)]
    across = swap((far[0].astype(F32) + of_tp(t ^ 2)).astype(BF), 2)
    act = gated(far[1].astype(F32) + of_tp(t) + across.astype(F32), row_scale)
    shared_acts = jnp.stack(over_tp(act))
    shared_acts = jnp.concatenate(
        [lax.dynamic_index_in_dim(shared_acts, t ^ q, 0, keepdims=False) for q in range(4)], axis=1
    )
    shared_rows = jnp.zeros((4, 4, down_row.shape[1], width), BF)
    for by, piece in {0: down_row, **down_lines}.items():
        shared_rows = lax.dynamic_update_slice(
            shared_rows, piece[:, None], (0, (x - by) % 4, 0, 0)
        )
    shared = product(shared_acts, shared_rows.reshape(-1, width))

    returned, shared = together(returned, shared)
    routed = lax.dot_general(
        combine,
        returned.reshape(ep * capacity, width),
        (((0,), (0,)), ((), ())),
        preferred_element_type=F32,
    )
    return (projected.astype(F32) + routed + shared).astype(BF)


def solution(mesh):
    finer = Mesh(mesh.devices.reshape(mesh.shape["tp"], 4, 4, 2), ("tp", "ep_0", "ep_1", "ep_2"))
    in_specs = (
        P(EP, "tp"),
        P(EP),
        P(EP, "tp"),
        P(),
        P(),
        P("tp"),
        P(None, EP, "tp"),
        P(EP, None),
        P(EP, None),
        P(EP, "tp", None, None),
        P(EP, None, "tp"),
        P(TP_EP, None, None),
        P(EP, "tp"),
    )
    out_specs = P(EP, "tp")

    def body(*args):
        args = list(args)
        args[9] = args[9].reshape(args[9].shape[1:])
        return on_device(*args)

    return jax.shard_map(body, mesh=finer, in_specs=in_specs, out_specs=out_specs, check_vma=False)
```

profile of v0, /device:TPU:2, one launch (start us, length us, event | category | flops | bytes accessed | tf_op | source)
XLA Modules:
  0.0 478.3 jit_solution(4188733497817455123)
XLA Ops:
  10.0 10.6 %all-to-all-start = ((s32[32,16,128]{2,1,0:T(8,128)}), s32[32,16,128]{2,1,0:T(8,128)S(1)}, u32[]{:S(2)}, u32[]{:S(2)}) async-start(s32[32,16,128]{2,1,0:T(8,128)} %pad_add_fusion), calls=%async_computation | async-start | bytes 524288 | tf_op jit(solution)/shard_map/all_to_all | solution.py:228
  24.9 5.4 %all-to-all-done.i_ref.p_ref = s32[32,16,128]{2,1,0:T(8,128)S(1)} async-done(((s32[32,16,128]{2,1,0:T(8,128)}), s32[32,16,128]{2,1,0:T(8,128)S(1)}, u32[]{:S(2)}, u32[]{:S(2)}) %all-to-all-start) | async-done | bytes 262176 | tf_op jit(solution)/shard_map/all_to_all | solution.py:228
  30.4 5.5 %all-to-all-start.1 = ((bf16[8,128,256]{2,1,0:T(8,128)(2,1)}), bf16[8,128,256]{2,1,0:T(8,128)(2,1)}, u32[]{:S(2)}, u32[]{:S(2)}) async-start(bf16[8,128,256]{2,1,0:T(8,128)(2,1)} %shard_map.128), calls=%async_computation.1 | async-start | bytes 1048576 | tf_op jit(solution)/shard_map/all_to_all | solution.py:258
  42.6 6.9 %shard_map.127 = bf16[4,8,64,256]{3,2,1,0:T(8,128)(2,1)} custom-call(s32[32,16,128]{2,1,0:T(8,128)} %copy-done.4, bf16[2048,1792]{1,0:T(8,128)(2,1)} %t_ref.1, f32[1,2048]{1,0:T(1,128)} %bitcast.201, f32[1,1792]{1,0:T(1,128)} %broadcast_in_dim.182.g_ref), custom_call_target="tpu_custom_call" | custom-call | flops 1879048192 | bytes 7340032 | tf_op jit(solution)/shard_map/pallas_call | solution.py:104
  49.5 7.4 %all-to-all-start.2 = ((bf16[32,64,256]{2,1,0:T(8,128)(2,1)}), bf16[32,64,256]{2,1,0:T(8,128)(2,1)S(1)}, u32[]{:S(2)}, u32[]{:S(2)}) async-start(bf16[32,64,256]{2,1,0:T(8,128)(2,1)} %bitcast.184), calls=%async_computation.2 | async-start | bytes 2097152 | tf_op jit(solution)/shard_map/all_to_all | solution.py:286
  74.2 5.8 %shard_map.129 = bf16[8,128,256]{2,1,0:T(8,128)(2,1)} custom-call(s32[1]{0:T(128)} %bitcast.f_ref, bf16[32,64,256]{2,1,0:T(8,128)(2,1)} %copy-done, s32[32,16,128]{2,1,0:T(8,128)} %copy-done.4), custom_call_target="tpu_custom_call" | custom-call | flops 134217728 | bytes 2097152 | tf_op jit(solution)/shard_map/pallas_call | solution.py:135
  80.0 7.2 %collective-permute-done.18 = bf16[56,2,1024]{2,1,0:T(2,128)(2,1)S(1)} collective-permute-done((bf16[56,2,1024]{2,1,0:T(2,128)(2,1)S(1)}, bf16[56,2,1024]{2,1,0:T(2,128)(2,1)S(1)}, u32[]{:S(2)}, u32[]{:S(2)}) %collective-permute-start.18) | collective-permute-done | bytes 229408 | tf_op jit(solution)/shard_map/ppermute | solution.py:30
  98.6 10.8 %collective-permute-done.11 = bf16[224,1792]{1,0:T(8,128)(2,1)S(1)} collective-permute-done((bf16[224,1792]{1,0:T(8,128)(2,1)S(1)}, bf16[224,1792]{1,0:T(8,128)(2,1)S(1)}, u32[]{:S(2)}, u32[]{:S(2)}) %collective-permute-start.11) | collective-permute-done | bytes 802848 | tf_op jit(solution)/shard_map/ppermute | solution.py:30
  114.3 6.4 %convolution_convert_fusion.4 = bf16[1024,1792]{1,0:T(8,128)(2,1)S(1)} fusion(bf16[1024,1792]{1,0:T(8,128)(2,1)} %bitcast.14, bf16[1024,256]{1,0:T(8,128)(2,1)S(1)} %collective-permute-done.8, bf16[1024,256]{1,0:T(8,128)(2,1)} %collective-permute-done.7, bf16[1024,256]{1,0:T(8,128)(2,1)S(1)} %collective-permute-done.6, bf16[1024,256]{1,0:T(8,128)(2,1)} %bitcast.8), kind=kOutput, calls=%fused_computation.15 | convolution fusion | flops 3768320000 | bytes 9437184 | tf_op jit(solution)/shard_map/dot_general | solution.py:181
  129.4 12.6 %collective-permute-done.13 = bf16[224,1792]{1,0:T(8,128)(2,1)S(1)} collective-permute-done((bf16[224,1792]{1,0:T(8,128)(2,1)S(1)}, bf16[224,1792]{1,0:T(8,128)(2,1)S(1)}, u32[]{:S(2)}, u32[]{:S(2)}) %collective-permute-start.13) | collective-permute-done | bytes 802848 | tf_op jit(solution)/shard_map/ppermute | solution.py:30
  145.1 7.5 %add_convert_fusion = bf16[1024,1792]{1,0:T(8,128)(2,1)} fusion(bf16[1024,1792]{1,0:T(8,128)(2,1)S(1)} %convolution_convert_fusion.4, bf16[1024,1792]{1,0:T(8,128)(2,1)} %bitcast.18, bf16[1024,256]{1,0:T(8,128)(2,1)S(1)} %collective-permute-done.4, bf16[1024,256]{1,0:T(8,128)(2,1)S(1)} %collective-permute-done.3, ...), kind=kOutput, calls=%fused_computation.12 | convolution fusion | flops 3771990016 | bytes 13107200 | tf_op jit(solution)/shard_map/dot_general | solution.py:181
  152.5 5.4 %all-to-all-start.3 = ((bf16[8,128,1792]{2,1,0:T(8,128)(2,1)}), bf16[8,128,1792]{2,1,0:T(8,128)(2,1)}, u32[]{:S(2)}, u32[]{:S(2)}) async-start(bf16[8,128,1792]{2,1,0:T(8,128)(2,1)} %bitcast.185), calls=%async_computation.3 | async-start | bytes 7340032 | tf_op jit(solution)/shard_map/all_to_all | solution.py:324
  166.3 13.0 %shard_map.130 = bf16[1792,1024]{1,0:T(8,128)(2,1)} custom-call(s32[2]{0:T(128)} %get-tuple-element.115.at, bf16[1792,2,1024]{2,1,0:T(2,128)(2,1)} %bitcast.174, f32[1792,1]{1,0:T(8,128)} %broadcast_in_dim.219.g_ref), custom_call_target="tpu_custom_call" | custom-call | flops 3670016 | bytes 7340032 | tf_op jit(solution)/shard_map/pallas_call | solution.py:163
  179.2 12.9 %shard_map.131 = bf16[1792,1024]{1,0:T(8,128)(2,1)} custom-call(s32[2]{0:T(128)} %get-tuple-element.116.at, bf16[1792,2,1024]{2,1,0:T(2,128)(2,1)} %bitcast.175, f32[1792,1]{1,0:T(8,128)} %broadcast_in_dim.219.g_ref), custom_call_target="tpu_custom_call" | custom-call | flops 3670016 | bytes 7340032 | tf_op jit(solution)/shard_map/pallas_call | solution.py:163
  196.4 10.4 %collective-permute-done.15 = bf16[64,1792]{1,0:T(8,128)(2,1)} collective-permute-done((bf16[64,1792]{1,0:T(8,128)(2,1)}, bf16[64,1792]{1,0:T(8,128)(2,1)}, u32[]{:S(2)}, u32[]{:S(2)}) %collective-permute-start.15) | collective-permute-done | bytes 229408 | tf_op jit(solution)/shard_map/ppermute | solution.py:30
  216.7 64.0 %all_to_all.30 = bf16[32,40,1792]{2,1,0:T(8,128)(2,1)S(1)} all-to-all(bf16[32,40,1792]{2,1,0:T(8,128)(2,1)S(1)} %bitcast.172), channel_id=1, replica_groups=mesh['tp'=4,'ep_0'=4,'ep_1'=4,'ep_2'=2] {'ep_0','ep_1','ep_2'}, dimensions={0} | all-to-all | bytes 9175040 | tf_op jit(solution)/shard_map/all_to_all | solution.py:336
  296.7 26.3 %collective-permute-done.27 = f32[10,128]{1,0:T(8,128)S(1)} collective-permute-done((f32[10,128]{1,0:T(8,128)S(1)}, f32[10,128]{1,0:T(8,128)S(1)}, u32[]{:S(2)}, u32[]{:S(2)}) %collective-permute-start.27) | collective-permute-done | bytes 5152 | tf_op jit(solution)/shard_map/ppermute | solution.py:25
  325.2 16.3 %collective-permute-done.29 = bf16[1280,256]{1,0:T(8,128)(2,1)} collective-permute-done((bf16[1280,256]{1,0:T(8,128)(2,1)}, bf16[1280,256]{1,0:T(8,128)(2,1)}, u32[]{:S(2)}, u32[]{:S(2)}) %collective-permute-start.29) | collective-permute-done | bytes 655392 | tf_op jit(solution)/shard_map/ppermute | solution.py:25
  351.8 13.2 %collective-permute-done.32 = bf16[4,64,1792]{2,1,0:T(8,128)(2,1)S(1)} collective-permute-done((bf16[4,64,1792]{2,1,0:T(8,128)(2,1)S(1)}, bf16[4,64,1792]{2,1,0:T(8,128)(2,1)S(1)}, u32[]{:S(2)}, u32[]{:S(2)}) %collective-permute-start.32) | collective-permute-done | bytes 917536 | tf_op jit(solution)/shard_map/ppermute | solution.py:30
  365.0 20.6 %collective-permute-done.34 = bf16[4,64,1792]{2,1,0:T(8,128)(2,1)S(1)} collective-permute-done((bf16[4,64,1792]{2,1,0:T(8,128)(2,1)S(1)}, bf16[4,64,1792]{2,1,0:T(8,128)(2,1)S(1)}, u32[]{:S(2)}, u32[]{:S(2)}) %collective-permute-start.34) | collective-permute-done | bytes 917536 | tf_op jit(solution)/shard_map/ppermute | solution.py:30
  385.6 6.5 %convolution_convert_fusion = bf16[1280,1792]{1,0:T(8,128)(2,1)} fusion(bf16[1280,1024]{1,0:T(8,128)(2,1)S(1)} %pad_maximum_fusion.1, bf16[1024,1792]{1,0:T(8,128)(2,1)S(1)} %copy-done.1), kind=kOutput, calls=%fused_computation.2 | convolution fusion | flops 4699914240 | bytes 10878976 | tf_op jit(solution)/shard_map/dot_general | solution.py:181
  398.2 6.4 %all-to-all-start.5 = ((bf16[32,40,1792]{2,1,0:T(8,128)(2,1)}), bf16[32,40,1792]{2,1,0:T(8,128)(2,1)}, u32[]{:S(2)}, u32[]{:S(2)}) async-start(bf16[32,40,1792]{2,1,0:T(8,128)(2,1)} %bitcast.183), calls=%async_computation.5 | async-start | bytes 9175040 | tf_op jit(solution)/shard_map/all_to_all | solution.py:370
  420.0 13.5 %collective-permute-done.37 = bf16[128,512]{0,1:T(8,128)(2,1)S(1)} collective-permute-done((bf16[128,512]{0,1:T(8,128)(2,1)S(1)}, bf16[128,512]{0,1:T(8,128)(2,1)S(1)}, u32[]{:S(2)}, u32[]{:S(2)}) %collective-permute-start.37) | collective-permute-done | bytes 131104 | tf_op jit(solution)/shard_map/ppermute | solution.py:25
  442.3 32.0 %all-to-all-done.5 = bf16[32,40,1792]{2,1,0:T(8,128)(2,1)} async-done(((bf16[32,40,1792]{2,1,0:T(8,128)(2,1)}), bf16[32,40,1792]{2,1,0:T(8,128)(2,1)}, u32[]{:S(2)}, u32[]{:S(2)}) %all-to-all-start.5) | async-done | bytes 4587552 | tf_op jit(solution)/shard_map/all_to_all | solution.py:370
  (214 shorter events, 150.8 us)
Async XLA Ops:
  37.3 51.7 %collective-permute-start.9 = (bf16[224,1792]{1,0:T(8,128)(2,1)S(1)}, bf16[224,1792]{1,0:T(8,128)(2,1)}, u32[]{:S(2)}, u32[]{:S(2)}) collective-permute-start(bf16[224,1792]{1,0:T(8,128)(2,1)S(1)} %get-tuple-element.55), channel_id=1, source_target_pairs={{0,8},{8,16},{16,24},{24,0},{1,9},{9,17},{17,25},{25,1},{2,10},{10... | collective-permute-start | bytes 2408456 | tf_op jit(solution)/shard_map/ppermute | solution.py:30
  37.4 51.6 %collective-permute-start.10 = (bf16[224,1792]{1,0:T(8,128)(2,1)S(1)}, bf16[224,1792]{1,0:T(8,128)(2,1)}, u32[]{:S(2)}, u32[]{:S(2)}) collective-permute-start(bf16[224,1792]{1,0:T(8,128)(2,1)S(1)} %get-tuple-element.55), channel_id=1, source_target_pairs={{0,24},{8,0},{16,8},{24,16},{1,25},{9,1},{17,9},{25,17},{2,26},{10... | collective-permute-start | bytes 2408456 | tf_op jit(solution)/shard_map/ppermute | solution.py:30
  49.5 23.7 %all-to-all-start.2 = ((bf16[32,64,256]{2,1,0:T(8,128)(2,1)}), bf16[32,64,256]{2,1,0:T(8,128)(2,1)S(1)}, u32[]{:S(2)}, u32[]{:S(2)}) async-start(bf16[32,64,256]{2,1,0:T(8,128)(2,1)} %bitcast.184), calls=%async_computation.2 | async-start | bytes 2097152 | tf_op jit(solution)/shard_map/all_to_all | solution.py:286
  59.9 31.2 %collective-permute-start.7 = (bf16[1024,256]{1,0:T(8,128)(2,1)}, bf16[1024,256]{1,0:T(8,128)(2,1)}, u32[]{:S(2)}, u32[]{:S(2)}) collective-permute-start(bf16[1024,256]{1,0:T(8,128)(2,1)} %bitcast.8), channel_id=1, source_target_pairs={{0,64},{32,96},{64,0},{96,32},{1,65},{33,97},{65,1},{97,33},{2,66}... | collective-permute-start | bytes 1572872 | tf_op jit(solution)/shard_map/ppermute | solution.py:25
  61.9 25.2 %collective-permute-start.18 = (bf16[56,2,1024]{2,1,0:T(2,128)(2,1)S(1)}, bf16[56,2,1024]{2,1,0:T(2,128)(2,1)S(1)}, u32[]{:S(2)}, u32[]{:S(2)}) collective-permute-start(bf16[56,2,1024]{2,1,0:T(2,128)(2,1)S(1)} %copy-done.13), channel_id=1, source_target_pairs={{0,1},{1,0},{2,3},{3,2},{4,5},{5,4},{6,7},{7,6},{8,9},{9,8},{10,11... | collective-permute-start | bytes 688136 | tf_op jit(solution)/shard_map/ppermute | solution.py:30
  65.3 25.7 %collective-permute-start.14 = (bf16[32,1792]{1,0:T(8,128)(2,1)S(1)}, bf16[32,1792]{1,0:T(8,128)(2,1)S(1)}, u32[]{:S(2)}, u32[]{:S(2)}) collective-permute-start(bf16[32,1792]{1,0:T(8,128)(2,1)S(1)} %copy-done.15), channel_id=1, source_target_pairs={{0,1},{1,0},{2,3},{3,2},{4,5},{5,4},{6,7},{7,6},{8,9},{9,8},{10,11... | collective-permute-start | bytes 344072 | tf_op jit(solution)/shard_map/ppermute | solution.py:30
  89.0 36.9 %collective-permute-start.12 = (bf16[224,1792]{1,0:T(8,128)(2,1)S(1)}, bf16[224,1792]{1,0:T(8,128)(2,1)S(1)}, u32[]{:S(2)}, u32[]{:S(2)}) collective-permute-start(bf16[224,1792]{1,0:T(8,128)(2,1)S(1)} %get-tuple-element.54), channel_id=1, source_target_pairs={{0,24},{8,0},{16,8},{24,16},{1,25},{9,1},{17,9},{25,17},{2,26},{10... | collective-permute-start | bytes 2408456 | tf_op jit(solution)/shard_map/ppermute | solution.py:30
  91.0 36.5 %collective-permute-start.5 = (bf16[224,1792]{1,0:T(8,128)(2,1)S(1)}, bf16[224,1792]{1,0:T(8,128)(2,1)S(1)}, u32[]{:S(2)}, u32[]{:S(2)}) collective-permute-start(bf16[224,1792]{1,0:T(8,128)(2,1)S(1)} %get-tuple-element.54), channel_id=1, source_target_pairs={{0,8},{8,16},{16,24},{24,0},{1,9},{9,17},{17,25},{25,1},{2,10},{10... | collective-permute-start | bytes 2408456 | tf_op jit(solution)/shard_map/ppermute | solution.py:30
  109.5 32.6 %collective-permute-start.13 = (bf16[224,1792]{1,0:T(8,128)(2,1)S(1)}, bf16[224,1792]{1,0:T(8,128)(2,1)S(1)}, u32[]{:S(2)}, u32[]{:S(2)}) collective-permute-start(bf16[224,1792]{1,0:T(8,128)(2,1)S(1)} %get-tuple-element.54), channel_id=1, source_target_pairs={{0,16},{8,24},{16,0},{24,8},{1,17},{9,25},{17,1},{25,9},{2,18},{10... | collective-permute-start | bytes 2408456 | tf_op jit(solution)/shard_map/ppermute | solution.py:30
  112.3 31.3 %collective-permute-start.19 = (bf16[112,2,1024]{2,1,0:T(2,128)(2,1)S(1)}, bf16[112,2,1024]{2,1,0:T(2,128)(2,1)S(1)}, u32[]{:S(2)}, u32[]{:S(2)}) collective-permute-start(bf16[112,2,1024]{2,1,0:T(2,128)(2,1)S(1)} %broadcast_select_fusion.1), channel_id=1, source_target_pairs={{0,2},{2,4},{4,6},{6,0},{1,3},{3,5},{5,7},{7,1},{8,10},{10,12},{12... | collective-permute-start | bytes 1376264 | tf_op jit(solution)/shard_map/ppermute | solution.py:30
  113.3 30.5 %collective-permute-start.20 = (bf16[112,2,1024]{2,1,0:T(2,128)(2,1)S(1)}, bf16[112,2,1024]{2,1,0:T(2,128)(2,1)S(1)}, u32[]{:S(2)}, u32[]{:S(2)}) collective-permute-start(bf16[112,2,1024]{2,1,0:T(2,128)(2,1)S(1)} %broadcast_select_fusion.1), channel_id=1, source_target_pairs={{0,6},{2,0},{4,2},{6,4},{1,7},{3,1},{5,3},{7,5},{8,14},{10,8},{12,... | collective-permute-start | bytes 1376264 | tf_op jit(solution)/shard_map/ppermute | solution.py:30
  152.5 60.1 %all-to-all-start.3 = ((bf16[8,128,1792]{2,1,0:T(8,128)(2,1)}), bf16[8,128,1792]{2,1,0:T(8,128)(2,1)}, u32[]{:S(2)}, u32[]{:S(2)}) async-start(bf16[8,128,1792]{2,1,0:T(8,128)(2,1)} %bitcast.185), calls=%async_computation.3 | async-start | bytes 7340032 | tf_op jit(solution)/shard_map/all_to_all | solution.py:324
  158.1 54.5 %collective-permute-start.22 = (bf16[448,2,1024]{2,0,1:T(8,128)(2,1)S(1)}, bf16[448,2,1024]{2,0,1:T(8,128)(2,1)}, u32[]{:S(2)}, u32[]{:S(2)}) collective-permute-start(bf16[448,2,1024]{2,0,1:T(8,128)(2,1)S(1)} %bitcast.179), channel_id=1, source_target_pairs={{0,8},{8,16},{16,24},{24,0},{1,9},{9,17},{17,25},{25,1},{2,10},{10... | collective-permute-start | bytes 5505032 | tf_op jit(solution)/shard_map/ppermute | solution.py:30
  159.3 53.3 %collective-permute-start.23 = (bf16[448,2,1024]{2,0,1:T(8,128)(2,1)S(1)}, bf16[448,2,1024]{2,0,1:T(8,128)(2,1)}, u32[]{:S(2)}, u32[]{:S(2)}) collective-permute-start(bf16[448,2,1024]{2,0,1:T(8,128)(2,1)S(1)} %bitcast.180), channel_id=1, source_target_pairs={{0,24},{8,0},{16,8},{24,16},{1,25},{9,1},{17,9},{25,17},{2,26},{10... | collective-permute-start | bytes 5505032 | tf_op jit(solution)/shard_map/ppermute | solution.py:30
  161.4 45.5 %collective-permute-start.15 = (bf16[64,1792]{1,0:T(8,128)(2,1)}, bf16[64,1792]{1,0:T(8,128)(2,1)}, u32[]{:S(2)}, u32[]{:S(2)}) collective-permute-start(bf16[64,1792]{1,0:T(8,128)(2,1)} %maximum_select_fusion), channel_id=1, source_target_pairs={{0,8},{8,16},{16,24},{24,0},{1,9},{9,17},{17,25},{25,1},{2,10},{10... | collective-permute-start | bytes 688136 | tf_op jit(solution)/shard_map/ppermute | solution.py:30
  161.4 49.2 %collective-permute-start.16 = (bf16[64,1792]{1,0:T(8,128)(2,1)}, bf16[64,1792]{1,0:T(8,128)(2,1)S(1)}, u32[]{:S(2)}, u32[]{:S(2)}) collective-permute-start(bf16[64,1792]{1,0:T(8,128)(2,1)} %maximum_select_fusion), channel_id=1, source_target_pairs={{0,24},{8,0},{16,8},{24,16},{1,25},{9,1},{17,9},{25,17},{2,26},{10... | collective-permute-start | bytes 688136 | tf_op jit(solution)/shard_map/ppermute | solution.py:30
  164.6 47.0 %collective-permute-start.17 = (bf16[64,1792]{1,0:T(8,128)(2,1)}, bf16[64,1792]{1,0:T(8,128)(2,1)S(1)}, u32[]{:S(2)}, u32[]{:S(2)}) collective-permute-start(bf16[64,1792]{1,0:T(8,128)(2,1)} %maximum_select_fusion), channel_id=1, source_target_pairs={{0,16},{8,24},{16,0},{24,8},{1,17},{9,25},{17,1},{25,9},{2,18},{10... | collective-permute-start | bytes 688136 | tf_op jit(solution)/shard_map/ppermute | solution.py:30
  291.6 31.4 %collective-permute-start.25 = (bf16[1280,512]{1,0:T(8,128)(2,1)S(1)}, bf16[1280,512]{1,0:T(8,128)(2,1)S(1)}, u32[]{:S(2)}, u32[]{:S(2)}) collective-permute-start(bf16[1280,512]{1,0:T(8,128)(2,1)S(1)} %add_convert_fusion.1), channel_id=1, source_target_pairs={{0,64},{32,96},{64,0},{96,32},{1,65},{33,97},{65,1},{97,33},{2,66}... | collective-permute-start | bytes 3932168 | tf_op jit(solution)/shard_map/ppermute | solution.py:25
  294.2 28.8 %collective-permute-start.27 = (f32[10,128]{1,0:T(8,128)S(1)}, f32[10,128]{1,0:T(8,128)S(1)}, u32[]{:S(2)}, u32[]{:S(2)}) collective-permute-start(f32[10,128]{1,0:T(8,128)S(1)} %bitcast_add_fusion.3), channel_id=1, source_target_pairs={{0,64},{32,96},{64,0},{96,32},{1,65},{33,97},{65,1},{97,33},{2,66}... | collective-permute-start | bytes 15368 | tf_op jit(solution)/shard_map/ppermute | solution.py:25
  295.9 55.9 %collective-permute-start.31 = (bf16[448,2,1024]{2,0,1:T(8,128)(2,1)S(1)}, bf16[448,2,1024]{2,0,1:T(8,128)(2,1)}, u32[]{:S(2)}, u32[]{:S(2)}) collective-permute-start(bf16[448,2,1024]{2,0,1:T(8,128)(2,1)S(1)} %bitcast.181), channel_id=1, source_target_pairs={{0,16},{8,24},{16,0},{24,8},{1,17},{9,25},{17,1},{25,9},{2,18},{10... | collective-permute-start | bytes 5505032 | tf_op jit(solution)/shard_map/ppermute | solution.py:30
  341.7 23.3 %collective-permute-start.32 = (bf16[4,64,1792]{2,1,0:T(8,128)(2,1)S(1)}, bf16[4,64,1792]{2,1,0:T(8,128)(2,1)S(1)}, u32[]{:S(2)}, u32[]{:S(2)}) collective-permute-start(bf16[4,64,1792]{2,1,0:T(8,128)(2,1)S(1)} %bitcast_dynamic-update-slice_fusion.16), channel_id=1, source_target_pairs={{0,2},{2,4},{4,6},{6,0},{1,3},{3,5},{5,7},{7,1},{8,10},{10,12},{12... | collective-permute-start | bytes 2752520 | tf_op jit(solution)/shard_map/ppermute | solution.py:30
  343.8 41.8 %collective-permute-start.34 = (bf16[4,64,1792]{2,1,0:T(8,128)(2,1)S(1)}, bf16[4,64,1792]{2,1,0:T(8,128)(2,1)S(1)}, u32[]{:S(2)}, u32[]{:S(2)}) collective-permute-start(bf16[4,64,1792]{2,1,0:T(8,128)(2,1)S(1)} %bitcast_dynamic-update-slice_fusion.16), channel_id=1, source_target_pairs={{0,4},{2,6},{4,0},{6,2},{1,5},{3,7},{5,1},{7,3},{8,12},{10,14},{12... | collective-permute-start | bytes 2752520 | tf_op jit(solution)/shard_map/ppermute | solution.py:30
  392.3 23.9 %collective-permute-start.38 = (f32[1,128]{1,0:T(1,128)S(1)}, f32[1,128]{1,0:T(1,128)S(1)}, u32[]{:S(2)}, u32[]{:S(2)}) collective-permute-start(f32[1,128]{1,0:T(1,128)S(1)} %bitcast.202), channel_id=1, source_target_pairs={{0,32},{32,0},{64,96},{96,64},{1,33},{33,1},{65,97},{97,65},{2,34}... | collective-permute-start | bytes 1544 | tf_op jit(solution)/shard_map/ppermute | solution.py:25
  398.2 76.0 %all-to-all-start.5 = ((bf16[32,40,1792]{2,1,0:T(8,128)(2,1)}), bf16[32,40,1792]{2,1,0:T(8,128)(2,1)}, u32[]{:S(2)}, u32[]{:S(2)}) async-start(bf16[32,40,1792]{2,1,0:T(8,128)(2,1)} %bitcast.183), calls=%async_computation.5 | async-start | bytes 9175040 | tf_op jit(solution)/shard_map/all_to_all | solution.py:370
  (43 other events, 598.0 us)
where the time goes:
time: 487 us; the launch traced here: 478 us
  waiting for transfers between devices  189 us (39%)
  starting transfers between devices  73.4 us (15%)
  blocking collectives  64 us (13%)
  matrix products  43.2 us (9%)
  local copies, waits for them, and re-layouts  41.6 us (9%)
  Pallas kernels  40.7 us (8%)
  other arithmetic  25.2 us (5%)
    ppermute x20, waiting for transfers between devices, shift(): lax.ppermute(value, axis, [(i, (i + by) % size) for i in range(size)])  83.7 us
    all_to_all x1, blocking collectives, on_device(): lax.all_to_all(outgoing.reshape(ep, capacity, width), EP, split_axis=0, c...  64 us
    ppermute x23, waiting for transfers between devices, swap(): return lax.ppermute(value, 'tp', [(i, i ^ bit) for i in range(4)])  63.7 us
    dot_general x7, matrix products, product(): return jnp.dot(rows, weights, preferred_element_type=F32)  37.5 us
    all_to_all x1, waiting for transfers between devices, on_device(): lax.all_to_all(result.reshape(ep, capacity, width), EP, split_axis=0, con...  32 us
    ppermute x20, starting transfers between devices, shift(): lax.ppermute(value, axis, [(i, (i + by) % size) for i in range(size)])  27.3 us
    pallas_call x2, Pallas kernels, gained_columns(): pl.pallas_call(kernel, grid_spec=pltpu.PrefetchScalarGridSpec(num_scalar_...  25.9 us
    ppermute x23, starting transfers between devices, swap(): return lax.ppermute(value, 'tp', [(i, i ^ bit) for i in range(4)])  10.7 us
  transfers between devices with their start and end apart: 48, of which 21 were waited for; matrix products, arithmetic and copies ran while one was open for 16% of the time, Pallas kernels for 9%

commit v1 on v0

--- a/solution.py
+++ b/solution.py
@@ -210,7 +210,6 @@
     model = width * 4
     t = lax.axis_index("tp")
     y = lax.axis_index("ep_0")
-    x = lax.axis_index("ep_1")
     z = lax.axis_index("ep_2")
     experts = jnp.arange(ep, dtype=jnp.int32)
 
@@ -237,7 +236,7 @@
             whole = lax.dynamic_update_slice(whole, piece[None], (t ^ ((y - by) % 4), 0, 0))
         return whole.reshape(-1, width)
 
-    hidden_pieces = moved(0, asked, (1, 3, 2))
+    hidden_pieces = moved(0, asked, (1, 3))
 
     wide_hidden = after(hidden_in, asked).astype(F32)
     wide_table = after(embed_table, asked).astype(F32)
@@ -262,7 +261,8 @@
 
     found = found_blocks(ids, embed_table, scales[None, :vocab], embed_gain, planes, plane)
     found = after(found.reshape(ep, plane * id_slots, -1), blocks)
-    embed_pieces = moved(1, found, (1, 3, 2))
+    hidden_pieces[2] = shift(after(hidden_pieces[1], found), "ep_0", 1)
+    embed_pieces = moved(1, found, (1, 3))
     gain_column = ffn_gain[:, None]
 
     def columns(which, gate):
@@ -287,6 +287,7 @@
     first = (y * plane).astype(jnp.int32).reshape(1)
     embed_blocks = picked_blocks(first, found, ids, plane, tokens)
     embed_acts = side_by_side(embed_blocks)
+    embed_pieces[2] = shift(after(embed_pieces[3], embed_blocks), "ep_0", 3)
     hidden_acts = side_by_side(blocks)
     for by in (1, 3, 2):
         hidden_pieces[by] = after(hidden_pieces[by], embed_blocks)
@@ -294,6 +295,7 @@
     gate_up_row = of_pair(*gate_up_row, embed_blocks)
     down_row = of_pair(*down_row, embed_blocks)
     gate_up_row = of_line(gate_up_row, "ep_1")
+    down_row = of_line(down_row, "ep_1")
     gate_up_row = gate_up_row.reshape(-1, *shared_gate_up.shape[1:])
     for by in (1, 3, 2):
         embed_pieces[by] = after(embed_pieces[by], start)
@@ -318,17 +320,16 @@
         [lax.dynamic_index_in_dim(down_block, t ^ q, 0, keepdims=False) for q in range(4)]
     )
 
-    gate_up_row = after(gate_up_row, partial)
+    gate_up_row, down_row, _ = together(gate_up_row, down_row, partial)
     gate_up_lines = {by: shift(gate_up_row, "ep_0", by) for by in (1, 3)}
-    down_row = of_line(after(down_row, partial), "ep_0")
     sums = lax.all_to_all(
         partial.reshape(plane, tokens, width), XZ, split_axis=0, concat_axis=0, tiled=True
     )
     sums, far_columns, near_columns, down_block, send, combine = together(
         sums, far_columns, near_columns, down_block, send, combine
     )
-    sums, down_row, gate_up_lines[1], gate_up_lines[3] = together(
-        sums, down_row, gate_up_lines[1], gate_up_lines[3]
+    sums, gate_up_lines[1], gate_up_lines[3] = together(
+        sums, gate_up_lines[1], gate_up_lines[3]
     )
     projected = sums.astype(F32).sum(axis=0).astype(BF)
 
@@ -345,7 +346,7 @@
     rows = arrived.reshape(ep * capacity, width)
     gate_up_lines[2] = shift(after(gate_up_row, arrived), "ep_0", 2)
     down_row = after(down_row, arrived)
-    down_lines = {by: shift(down_row, "ep_1", by) for by in (1, 3, 2)}
+    down_lines = {by: shift(down_row, "ep_0", by) for by in (1, 3, 2)}
     far = product(rows, far_columns).astype(BF)
     far = swap(far, 1)
     near = product(rows, near_columns).astype(BF)
@@ -363,9 +364,6 @@
     across = swap(across, 2)
     act = gated(both(far, near, 1) + across.astype(F32), slot_scale)
     acts = jnp.concatenate(over_tp(act), axis=1)
-    acts, gate_up_lines[2] = together(acts, gate_up_lines[2])
-    for by in (1, 3, 2):
-        acts, down_lines[by] = together(acts, down_lines[by])
     result = product(acts, down_block).astype(BF)
     returned = lax.all_to_all(
         result.reshape(ep, capacity, width), EP, split_axis=0, concat_axis=0, tiled=True
@@ -378,6 +376,9 @@
     row_scale = lax.rsqrt(squares / model + 1e-06).reshape(tokens, 1)
 
     gate_up_row, down_row = after(gate_up_row, result), after(down_row, result)
+    for lines in (gate_up_lines, down_lines):
+        for by in list(lines):
+            lines[by] = after(lines[by], result)
     shared_columns = stacked(gate_up_row, "ep_0", gate_up_lines).reshape(width, 2, -1)
     shared_columns = jnp.concatenate(
         [(shared_columns[:, j].astype(F32) * gain_column).astype(BF) for j in range(2)], axis=1
@@ -398,11 +399,7 @@
     shared_acts = jnp.concatenate(
         [lax.dynamic_index_in_dim(shared_acts, t ^ q, 0, keepdims=False) for q in range(4)], axis=1
     )
-    shared_rows = jnp.zeros((4, 4, down_row.shape[1], width), BF)
-    for by, piece in {0: down_row, **down_lines}.items():
-        shared_rows = lax.dynamic_update_slice(
-            shared_rows, piece[:, None], (0, (x - by) % 4, 0, 0)
-        )
+    shared_rows = stacked(down_row, "ep_0", down_lines)
     shared = product(shared_acts, shared_rows.reshape(-1, width))
 
     returned, shared = together(returned, shared)

time: 487 us -> 508 us (1.043)
  the two profiles are of different devices: /device:TPU:2 before, /device:TPU:1 now
where the time goes in v1:
time: 508 us; the launch traced here: 499 us
  waiting for transfers between devices  213 us (42%)
  starting transfers between devices  79.7 us (16%)
  blocking collectives  59.4 us (12%)
  matrix products  41.6 us (8%)
  local copies, waits for them, and re-layouts  40.9 us (8%)
  Pallas kernels  40.8 us (8%)
  other arithmetic  23 us (5%)
    ppermute x20, waiting for transfers between devices, shift(): lax.ppermute(value, axis, [(i, (i + by) % size) for i in range(size)])  114 us
    all_to_all x1, blocking collectives, on_device(): lax.all_to_all(outgoing.reshape(ep, capacity, width), EP, split_axis=0, c...  59.4 us
    ppermute x23, waiting for transfers between devices, swap(): return lax.ppermute(value, 'tp', [(i, i ^ bit) for i in range(4)])  54.2 us
    dot_general x7, matrix products, product(): return jnp.dot(rows, weights, preferred_element_type=F32)  36 us
    all_to_all x1, waiting for transfers between devices, on_device(): lax.all_to_all(result.reshape(ep, capacity, width), EP, split_axis=0, con...  28.3 us
    pallas_call x2, Pallas kernels, gained_columns(): pl.pallas_call(kernel, grid_spec=pltpu.PrefetchScalarGridSpec(num_scalar_...  25.9 us
    ppermute x23, starting transfers between devices, swap(): return lax.ppermute(value, 'tp', [(i, i ^ bit) for i in range(4)])  24.9 us
    ppermute x20, starting transfers between devices, shift(): lax.ppermute(value, axis, [(i, (i + by) % size) for i in range(size)])  21.8 us
  transfers between devices with their start and end apart: 48, of which 21 were waited for; matrix products, arithmetic and copies ran while one was open for 16% of the time, Pallas kernels for 8%

profile of v1, /device:TPU:1, one launch (start us, length us, event | category | flops | bytes accessed | tf_op | source)
XLA Modules:
  0.0 499.0 jit_solution(11010539946299120957)
XLA Ops:
  11.8 10.1 %all-to-all-start = ((s32[32,16,128]{2,1,0:T(8,128)}), s32[32,16,128]{2,1,0:T(8,128)S(1)}, u32[]{:S(2)}, u32[]{:S(2)}) async-start(s32[32,16,128]{2,1,0:T(8,128)} %pad_add_fusion), calls=%async_computation | async-start | bytes 524288 | tf_op jit(solution)/shard_map/all_to_all | solution.py:227
  26.2 5.8 %all-to-all-done.i_ref.p_ref = s32[32,16,128]{2,1,0:T(8,128)S(1)} async-done(((s32[32,16,128]{2,1,0:T(8,128)}), s32[32,16,128]{2,1,0:T(8,128)S(1)}, u32[]{:S(2)}, u32[]{:S(2)}) %all-to-all-start) | async-done | bytes 262176 | tf_op jit(solution)/shard_map/all_to_all | solution.py:227
  38.1 6.9 %shard_map.127 = bf16[4,8,64,256]{3,2,1,0:T(8,128)(2,1)} custom-call(s32[32,16,128]{2,1,0:T(8,128)} %copy-done.5, bf16[2048,1792]{1,0:T(8,128)(2,1)} %t_ref.1, f32[1,2048]{1,0:T(1,128)} %bitcast.197, f32[1,1792]{1,0:T(1,128)} %broadcast_in_dim.181.g_ref), custom_call_target="tpu_custom_call" | custom-call | flops 1879048192 | bytes 7340032 | tf_op jit(solution)/shard_map/pallas_call | solution.py:104
  45.0 7.2 %all-to-all-start.2 = ((bf16[32,64,256]{2,1,0:T(8,128)(2,1)}), bf16[32,64,256]{2,1,0:T(8,128)(2,1)S(1)}, u32[]{:S(2)}, u32[]{:S(2)}) async-start(bf16[32,64,256]{2,1,0:T(8,128)(2,1)} %bitcast.177), calls=%async_computation.2 | async-start | bytes 2097152 | tf_op jit(solution)/shard_map/all_to_all | solution.py:286
  62.6 22.0 %collective-permute-done.9 = bf16[224,1792]{1,0:T(8,128)(2,1)} collective-permute-done((bf16[224,1792]{1,0:T(8,128)(2,1)S(1)}, bf16[224,1792]{1,0:T(8,128)(2,1)}, u32[]{:S(2)}, u32[]{:S(2)}) %collective-permute-start.9) | collective-permute-done | bytes 802848 | tf_op jit(solution)/shard_map/ppermute | solution.py:30
  86.3 5.8 %shard_map.129 = bf16[8,128,256]{2,1,0:T(8,128)(2,1)} custom-call(s32[1]{0:T(128)} %bitcast.f_ref, bf16[32,64,256]{2,1,0:T(8,128)(2,1)} %copy-done, s32[32,16,128]{2,1,0:T(8,128)} %copy-done.5), custom_call_target="tpu_custom_call" | custom-call | flops 134217728 | bytes 2097152 | tf_op jit(solution)/shard_map/pallas_call | solution.py:135
  102.5 9.2 %collective-permute-done.12 = bf16[224,1792]{1,0:T(8,128)(2,1)S(1)} collective-permute-done((bf16[224,1792]{1,0:T(8,128)(2,1)S(1)}, bf16[224,1792]{1,0:T(8,128)(2,1)S(1)}, u32[]{:S(2)}, u32[]{:S(2)}) %collective-permute-start.12) | collective-permute-done | bytes 802848 | tf_op jit(solution)/shard_map/ppermute | solution.py:30
  114.1 16.3 %collective-permute-done.11 = bf16[224,1792]{1,0:T(8,128)(2,1)S(1)} collective-permute-done((bf16[224,1792]{1,0:T(8,128)(2,1)}, bf16[224,1792]{1,0:T(8,128)(2,1)S(1)}, u32[]{:S(2)}, u32[]{:S(2)}) %collective-permute-start.11) | collective-permute-done | bytes 802848 | tf_op jit(solution)/shard_map/ppermute | solution.py:30
  133.5 6.6 %convolution_convert_fusion.4 = bf16[1024,1792]{1,0:T(8,128)(2,1)S(1)} fusion(bf16[1024,1792]{1,0:T(8,128)(2,1)} %bitcast.14, bf16[1024,256]{1,0:T(8,128)(2,1)S(1)} %collective-permute-done.8, bf16[1024,256]{1,0:T(8,128)(2,1)} %collective-permute-done.7, bf16[1024,256]{1,0:T(8,128)(2,1)} %collective-permute-done.6, bf16[1024,256]{1,0:T(8,128)(2,1)} %bitcast.8), kind=kOutput, calls=%fused_computation.15 | convolution fusion | flops 3768320000 | bytes 9437184 | tf_op jit(solution)/shard_map/dot_general | solution.py:181
  147.8 12.5 %collective-permute-done.13 = bf16[224,1792]{1,0:T(8,128)(2,1)S(1)} collective-permute-done((bf16[224,1792]{1,0:T(8,128)(2,1)S(1)}, bf16[224,1792]{1,0:T(8,128)(2,1)S(1)}, u32[]{:S(2)}, u32[]{:S(2)}) %collective-permute-start.13) | collective-permute-done | bytes 802848 | tf_op jit(solution)/shard_map/ppermute | solution.py:30
  164.3 5.4 %add_convert_fusion = bf16[1024,1792]{1,0:T(8,128)(2,1)} fusion(bf16[1024,1792]{1,0:T(8,128)(2,1)S(1)} %convolution_convert_fusion.4, bf16[1024,1792]{1,0:T(8,128)(2,1)S(1)} %bitcast.180, bf16[1024,256]{1,0:T(8,128)(2,1)S(1)} %collective-permute-done.4, bf16[1024,256]{1,0:T(8,128)(2,1)S(1)} %collective-permute-done.3, ...), kind=kOutput, calls=%fused_computation.12 | convolution fusion | flops 3771990016 | bytes 13107200 | tf_op jit(solution)/shard_map/dot_general | solution.py:181
  169.7 6.7 %all-to-all-start.3 = ((bf16[8,128,1792]{2,1,0:T(8,128)(2,1)}), bf16[8,128,1792]{2,1,0:T(8,128)(2,1)}, u32[]{:S(2)}, u32[]{:S(2)}) async-start(bf16[8,128,1792]{2,1,0:T(8,128)(2,1)} %bitcast.178), calls=%async_computation.3 | async-start | bytes 7340032 | tf_op jit(solution)/shard_map/all_to_all | solution.py:325
  187.3 13.0 %shard_map.131 = bf16[1792,1024]{1,0:T(8,128)(2,1)} custom-call(s32[2]{0:T(128)} %get-tuple-element.114.at, bf16[1792,2,1024]{2,1,0:T(2,128)(2,1)} %bitcast.167, f32[1792,1]{1,0:T(8,128)} %broadcast_in_dim.217.g_ref), custom_call_target="tpu_custom_call" | custom-call | flops 3670016 | bytes 7340032 | tf_op jit(solution)/shard_map/pallas_call | solution.py:163
  200.2 12.9 %shard_map.130 = bf16[1792,1024]{1,0:T(8,128)(2,1)} custom-call(s32[2]{0:T(128)} %get-tuple-element.113.at, bf16[1792,2,1024]{2,1,0:T(2,128)(2,1)} %bitcast.168, f32[1792,1]{1,0:T(8,128)} %broadcast_in_dim.217.g_ref), custom_call_target="tpu_custom_call" | custom-call | flops 3670016 | bytes 7340032 | tf_op jit(solution)/shard_map/pallas_call | solution.py:163
  217.5 10.5 %all-to-all-done.3 = bf16[8,128,1792]{2,1,0:T(8,128)(2,1)} async-done(((bf16[8,128,1792]{2,1,0:T(8,128)(2,1)}), bf16[8,128,1792]{2,1,0:T(8,128)(2,1)}, u32[]{:S(2)}, u32[]{:S(2)}) %all-to-all-start.3) | async-done | bytes 3670048 | tf_op jit(solution)/shard_map/all_to_all | solution.py:325
  232.1 59.4 %all_to_all.30 = bf16[32,40,1792]{2,1,0:T(8,128)(2,1)S(1)} all-to-all(bf16[32,40,1792]{2,1,0:T(8,128)(2,1)S(1)} %bitcast.165), channel_id=1, replica_groups=mesh['tp'=4,'ep_0'=4,'ep_1'=4,'ep_2'=2] {'ep_0','ep_1','ep_2'}, dimensions={0} | all-to-all | bytes 9175040 | tf_op jit(solution)/shard_map/all_to_all | solution.py:337
  291.5 5.1 %convolution_convert_fusion.3 = bf16[1280,1024]{1,0:T(8,128)(2,1)S(1)} fusion(bf16[1280,1792]{1,0:T(8,128)(2,1)S(1)} %bitcast.169, bf16[1792,1024]{1,0:T(8,128)(2,1)S(1)} %copy-done.2), kind=kOutput, calls=%fused_computation.14 | convolution fusion | flops 4698931200 | bytes 10878976 | tf_op jit(solution)/shard_map/dot_general | solution.py:181
  300.3 5.1 %convolution_convert_fusion.2 = bf16[1280,1024]{1,0:T(8,128)(2,1)S(1)} fusion(bf16[1280,1792]{1,0:T(8,128)(2,1)S(1)} %bitcast.170, bf16[1792,1024]{1,0:T(8,128)(2,1)S(1)} %copy-done.1), kind=kOutput, calls=%fused_computation.13 | convolution fusion | flops 4698931200 | bytes 10878976 | tf_op jit(solution)/shard_map/dot_general | solution.py:181
  309.8 26.8 %collective-permute-done.27 = f32[10,128]{1,0:T(8,128)S(1)} collective-permute-done((f32[10,128]{1,0:T(8,128)S(1)}, f32[10,128]{1,0:T(8,128)S(1)}, u32[]{:S(2)}, u32[]{:S(2)}) %collective-permute-start.27) | collective-permute-done | bytes 5152 | tf_op jit(solution)/shard_map/ppermute | solution.py:25
  341.1 13.0 %collective-permute-done.29 = bf16[1280,256]{1,0:T(8,128)(2,1)} collective-permute-done((bf16[1280,256]{1,0:T(8,128)(2,1)}, bf16[1280,256]{1,0:T(8,128)(2,1)}, u32[]{:S(2)}, u32[]{:S(2)}) %collective-permute-start.29) | collective-permute-done | bytes 655392 | tf_op jit(solution)/shard_map/ppermute | solution.py:25
  358.1 9.9 %convolution_convert_fusion = bf16[1280,1792]{1,0:T(8,128)(2,1)} fusion(bf16[1024,1792]{1,0:T(8,128)(2,1)} %pad_maximum_fusion, bf16[1280,256]{1,0:T(8,128)(2,1)} %collective-permute-done.30, bf16[1280,256]{1,0:T(8,128)(2,1)} %collective-permute-done.29, bf16[1280,256]{1,0:T(8,128)(2,1)} %collective-permute-done.28, bf16[1280,256]{1,0:T(8,128)(2,1)} %fusion.30), kind=kOutput, calls=%fused_computation.2 | convolution fusion | flops 4710400000 | bytes 10878976 | tf_op jit(solution)/shard_map/dot_general | solution.py:181
  368.0 32.8 %collective-permute-done.42 = bf16[4,64,1792]{2,1,0:T(8,128)(2,1)S(1)} collective-permute-done((bf16[4,64,1792]{2,1,0:T(8,128)(2,1)S(1)}, bf16[4,64,1792]{2,1,0:T(8,128)(2,1)S(1)}, u32[]{:S(2)}, u32[]{:S(2)}) %collective-permute-start.42) | collective-permute-done | bytes 917536 | tf_op jit(solution)/shard_map/ppermute | solution.py:30
  400.8 18.3 %collective-permute-done.41 = bf16[4,64,1792]{2,1,0:T(8,128)(2,1)S(1)} collective-permute-done((bf16[4,64,1792]{2,1,0:T(8,128)(2,1)S(1)}, bf16[4,64,1792]{2,1,0:T(8,128)(2,1)S(1)}, u32[]{:S(2)}, u32[]{:S(2)}) %collective-permute-start.41) | collective-permute-done | bytes 917536 | tf_op jit(solution)/shard_map/ppermute | solution.py:30
  466.6 28.3 %all-to-all-done.5 = bf16[32,40,1792]{2,1,0:T(8,128)(2,1)} async-done(((bf16[32,40,1792]{2,1,0:T(8,128)(2,1)}), bf16[32,40,1792]{2,1,0:T(8,128)(2,1)}, u32[]{:S(2)}, u32[]{:S(2)}) %all-to-all-start.5) | async-done | bytes 4587552 | tf_op jit(solution)/shard_map/all_to_all | solution.py:368
  (213 shorter events, 148.7 us)
Async XLA Ops:
  11.8 20.2 %all-to-all-start = ((s32[32,16,128]{2,1,0:T(8,128)}), s32[32,16,128]{2,1,0:T(8,128)S(1)}, u32[]{:S(2)}, u32[]{:S(2)}) async-start(s32[32,16,128]{2,1,0:T(8,128)} %pad_add_fusion), calls=%async_computation | async-start | bytes 524288 | tf_op jit(solution)/shard_map/all_to_all | solution.py:227
  45.0 40.3 %all-to-all-start.2 = ((bf16[32,64,256]{2,1,0:T(8,128)(2,1)}), bf16[32,64,256]{2,1,0:T(8,128)(2,1)S(1)}, u32[]{:S(2)}, u32[]{:S(2)}) async-start(bf16[32,64,256]{2,1,0:T(8,128)(2,1)} %bitcast.177), calls=%async_computation.2 | async-start | bytes 2097152 | tf_op jit(solution)/shard_map/all_to_all | solution.py:286
  53.8 39.9 %collective-permute-start.10 = (bf16[224,1792]{1,0:T(8,128)(2,1)S(1)}, bf16[224,1792]{1,0:T(8,128)(2,1)}, u32[]{:S(2)}, u32[]{:S(2)}) collective-permute-start(bf16[224,1792]{1,0:T(8,128)(2,1)S(1)} %get-tuple-element.54), channel_id=1, source_target_pairs={{0,24},{8,0},{16,8},{24,16},{1,25},{9,1},{17,9},{25,17},{2,26},{10... | collective-permute-start | bytes 2408456 | tf_op jit(solution)/shard_map/ppermute | solution.py:30
  56.3 28.3 %collective-permute-start.9 = (bf16[224,1792]{1,0:T(8,128)(2,1)S(1)}, bf16[224,1792]{1,0:T(8,128)(2,1)}, u32[]{:S(2)}, u32[]{:S(2)}) collective-permute-start(bf16[224,1792]{1,0:T(8,128)(2,1)S(1)} %get-tuple-element.54), channel_id=1, source_target_pairs={{0,8},{8,16},{16,24},{24,0},{1,9},{9,17},{17,25},{25,1},{2,10},{10... | collective-permute-start | bytes 2408456 | tf_op jit(solution)/shard_map/ppermute | solution.py:30
  56.3 37.4 %collective-permute-start.7 = (bf16[1024,256]{1,0:T(8,128)(2,1)}, bf16[1024,256]{1,0:T(8,128)(2,1)}, u32[]{:S(2)}, u32[]{:S(2)}) collective-permute-start(bf16[1024,256]{1,0:T(8,128)(2,1)} %bitcast.8), channel_id=1, source_target_pairs={{0,64},{32,96},{64,0},{96,32},{1,65},{33,97},{65,1},{97,33},{2,66}... | collective-permute-start | bytes 1572872 | tf_op jit(solution)/shard_map/ppermute | solution.py:25
  59.3 32.8 %collective-permute-start.18 = (bf16[32,1792]{1,0:T(8,128)(2,1)S(1)}, bf16[32,1792]{1,0:T(8,128)(2,1)S(1)}, u32[]{:S(2)}, u32[]{:S(2)}) collective-permute-start(bf16[32,1792]{1,0:T(8,128)(2,1)S(1)} %copy-done.15), channel_id=1, source_target_pairs={{0,1},{1,0},{2,3},{3,2},{4,5},{5,4},{6,7},{7,6},{8,9},{9,8},{10,11... | collective-permute-start | bytes 344072 | tf_op jit(solution)/shard_map/ppermute | solution.py:30
  62.1 30.6 %collective-permute-start.14 = (bf16[56,2,1024]{2,1,0:T(2,128)(2,1)S(1)}, bf16[56,2,1024]{2,1,0:T(2,128)(2,1)S(1)}, u32[]{:S(2)}, u32[]{:S(2)}) collective-permute-start(bf16[56,2,1024]{2,1,0:T(2,128)(2,1)S(1)} %copy-done.12), channel_id=1, source_target_pairs={{0,1},{1,0},{2,3},{3,2},{4,5},{5,4},{6,7},{7,6},{8,9},{9,8},{10,11... | collective-permute-start | bytes 688136 | tf_op jit(solution)/shard_map/ppermute | solution.py:30
  84.6 48.8 %collective-permute-start.6 = (bf16[1024,256]{1,0:T(8,128)(2,1)}, bf16[1024,256]{1,0:T(8,128)(2,1)}, u32[]{:S(2)}, u32[]{:S(2)}) collective-permute-start(bf16[1024,256]{1,0:T(8,128)(2,1)} %bitcast.8), channel_id=1, source_target_pairs={{0,32},{32,0},{64,96},{96,64},{1,33},{33,1},{65,97},{97,65},{2,34}... | collective-permute-start | bytes 1572872 | tf_op jit(solution)/shard_map/ppermute | solution.py:25
  92.8 47.4 %collective-permute-start.5 = (bf16[224,1792]{1,0:T(8,128)(2,1)S(1)}, bf16[224,1792]{1,0:T(8,128)(2,1)S(1)}, u32[]{:S(2)}, u32[]{:S(2)}) collective-permute-start(bf16[224,1792]{1,0:T(8,128)(2,1)S(1)} %get-tuple-element.53), channel_id=1, source_target_pairs={{0,8},{8,16},{16,24},{24,0},{1,9},{9,17},{17,25},{25,1},{2,10},{10... | collective-permute-start | bytes 2408456 | tf_op jit(solution)/shard_map/ppermute | solution.py:30
  93.7 36.6 %collective-permute-start.11 = (bf16[224,1792]{1,0:T(8,128)(2,1)}, bf16[224,1792]{1,0:T(8,128)(2,1)S(1)}, u32[]{:S(2)}, u32[]{:S(2)}) collective-permute-start(bf16[224,1792]{1,0:T(8,128)(2,1)} %collective-permute-done.9), channel_id=1, source_target_pairs={{0,8},{8,16},{16,24},{24,0},{1,9},{9,17},{17,25},{25,1},{2,10},{10... | collective-permute-start | bytes 2408456 | tf_op jit(solution)/shard_map/ppermute | solution.py:30
  93.8 39.6 %collective-permute-start.8 = (bf16[1024,256]{1,0:T(8,128)(2,1)}, bf16[1024,256]{1,0:T(8,128)(2,1)S(1)}, u32[]{:S(2)}, u32[]{:S(2)}) collective-permute-start(bf16[1024,256]{1,0:T(8,128)(2,1)} %collective-permute-done.7), channel_id=1, source_target_pairs={{0,32},{32,0},{64,96},{96,64},{1,33},{33,1},{65,97},{97,65},{2,34}... | collective-permute-start | bytes 1572872 | tf_op jit(solution)/shard_map/ppermute | solution.py:25
  111.7 64.8 %collective-permute-start.21 = (bf16[64,1792]{1,0:T(8,128)(2,1)}, bf16[64,1792]{1,0:T(8,128)(2,1)}, u32[]{:S(2)}, u32[]{:S(2)}) collective-permute-start(bf16[64,1792]{1,0:T(8,128)(2,1)} %maximum_select_fusion), channel_id=1, source_target_pairs={{0,4},{2,6},{4,0},{6,2},{1,5},{3,7},{5,1},{7,3},{8,12},{10,14},{12... | collective-permute-start | bytes 688136 | tf_op jit(solution)/shard_map/ppermute | solution.py:30
  140.1 24.1 %collective-permute-start.2 = (bf16[1024,256]{1,0:T(8,128)(2,1)S(1)}, bf16[1024,256]{1,0:T(8,128)(2,1)S(1)}, u32[]{:S(2)}, u32[]{:S(2)}) collective-permute-start(bf16[1024,256]{1,0:T(8,128)(2,1)S(1)} %bitcast.185), channel_id=1, source_target_pairs={{0,32},{32,0},{64,96},{96,64},{1,33},{33,1},{65,97},{97,65},{2,34}... | collective-permute-start | bytes 1572872 | tf_op jit(solution)/shard_map/ppermute | solution.py:25
  142.0 38.8 %collective-permute-start.17 = (bf16[112,2,1024]{2,1,0:T(2,128)(2,1)}, bf16[112,2,1024]{2,1,0:T(2,128)(2,1)}, u32[]{:S(2)}, u32[]{:S(2)}) collective-permute-start(bf16[112,2,1024]{2,1,0:T(2,128)(2,1)} %broadcast_select_fusion.1), channel_id=1, source_target_pairs={{0,4},{2,6},{4,0},{6,2},{1,5},{3,7},{5,1},{7,3},{8,12},{10,14},{12... | collective-permute-start | bytes 1376264 | tf_op jit(solution)/shard_map/ppermute | solution.py:30
  169.7 58.3 %all-to-all-start.3 = ((bf16[8,128,1792]{2,1,0:T(8,128)(2,1)}), bf16[8,128,1792]{2,1,0:T(8,128)(2,1)}, u32[]{:S(2)}, u32[]{:S(2)}) async-start(bf16[8,128,1792]{2,1,0:T(8,128)(2,1)} %bitcast.178), calls=%async_computation.3 | async-start | bytes 7340032 | tf_op jit(solution)/shard_map/all_to_all | solution.py:325
  182.0 46.0 %collective-permute-start.23 = (bf16[448,2,1024]{2,0,1:T(8,128)(2,1)S(1)}, bf16[448,2,1024]{2,0,1:T(8,128)(2,1)}, u32[]{:S(2)}, u32[]{:S(2)}) collective-permute-start(bf16[448,2,1024]{2,0,1:T(8,128)(2,1)S(1)} %bitcast.172), channel_id=1, source_target_pairs={{0,24},{8,0},{16,8},{24,16},{1,25},{9,1},{17,9},{25,17},{2,26},{10... | collective-permute-start | bytes 5505032 | tf_op jit(solution)/shard_map/ppermute | solution.py:30
  183.6 44.4 %collective-permute-start.22 = (bf16[448,2,1024]{2,0,1:T(8,128)(2,1)S(1)}, bf16[448,2,1024]{2,0,1:T(8,128)(2,1)}, u32[]{:S(2)}, u32[]{:S(2)}) collective-permute-start(bf16[448,2,1024]{2,0,1:T(8,128)(2,1)S(1)} %bitcast.173), channel_id=1, source_target_pairs={{0,8},{8,16},{16,24},{24,0},{1,9},{9,17},{17,25},{25,1},{2,10},{10... | collective-permute-start | bytes 5505032 | tf_op jit(solution)/shard_map/ppermute | solution.py:30
  306.0 30.6 %collective-permute-start.25 = (bf16[1280,512]{1,0:T(8,128)(2,1)S(1)}, bf16[1280,512]{1,0:T(8,128)(2,1)S(1)}, u32[]{:S(2)}, u32[]{:S(2)}) collective-permute-start(bf16[1280,512]{1,0:T(8,128)(2,1)S(1)} %add_convert_fusion.1), channel_id=1, source_target_pairs={{0,64},{32,96},{64,0},{96,32},{1,65},{33,97},{65,1},{97,33},{2,66}... | collective-permute-start | bytes 3932168 | tf_op jit(solution)/shard_map/ppermute | solution.py:25
  309.1 27.5 %collective-permute-start.27 = (f32[10,128]{1,0:T(8,128)S(1)}, f32[10,128]{1,0:T(8,128)S(1)}, u32[]{:S(2)}, u32[]{:S(2)}) collective-permute-start(f32[10,128]{1,0:T(8,128)S(1)} %bitcast_add_fusion.3), channel_id=1, source_target_pairs={{0,64},{32,96},{64,0},{96,32},{1,65},{33,97},{65,1},{97,33},{2,66}... | collective-permute-start | bytes 15368 | tf_op jit(solution)/shard_map/ppermute | solution.py:25
  339.2 82.8 %collective-permute-start.31 = (bf16[448,2,1024]{2,0,1:T(8,128)(2,1)S(1)}, bf16[448,2,1024]{2,0,1:T(8,128)(2,1)}, u32[]{:S(2)}, u32[]{:S(2)}) collective-permute-start(bf16[448,2,1024]{2,0,1:T(8,128)(2,1)S(1)} %bitcast.174), channel_id=1, source_target_pairs={{0,16},{8,24},{16,0},{24,8},{1,17},{9,25},{17,1},{25,9},{2,18},{10... | collective-permute-start | bytes 5505032 | tf_op jit(solution)/shard_map/ppermute | solution.py:30
  356.1 44.7 %collective-permute-start.42 = (bf16[4,64,1792]{2,1,0:T(8,128)(2,1)S(1)}, bf16[4,64,1792]{2,1,0:T(8,128)(2,1)S(1)}, u32[]{:S(2)}, u32[]{:S(2)}) collective-permute-start(bf16[4,64,1792]{2,1,0:T(8,128)(2,1)S(1)} %fusion.47), channel_id=1, source_target_pairs={{0,16},{8,24},{16,0},{24,8},{1,17},{9,25},{17,1},{25,9},{2,18},{10... | collective-permute-start | bytes 2752520 | tf_op jit(solution)/shard_map/ppermute | solution.py:30
  356.6 62.5 %collective-permute-start.41 = (bf16[4,64,1792]{2,1,0:T(8,128)(2,1)S(1)}, bf16[4,64,1792]{2,1,0:T(8,128)(2,1)S(1)}, u32[]{:S(2)}, u32[]{:S(2)}) collective-permute-start(bf16[4,64,1792]{2,1,0:T(8,128)(2,1)S(1)} %fusion.47), channel_id=1, source_target_pairs={{0,24},{8,0},{16,8},{24,16},{1,25},{9,1},{17,9},{25,17},{2,26},{10... | collective-permute-start | bytes 2752520 | tf_op jit(solution)/shard_map/ppermute | solution.py:30
  357.5 64.4 %collective-permute-start.40 = (bf16[4,64,1792]{2,1,0:T(8,128)(2,1)S(1)}, bf16[4,64,1792]{2,1,0:T(8,128)(2,1)S(1)}, u32[]{:S(2)}, u32[]{:S(2)}) collective-permute-start(bf16[4,64,1792]{2,1,0:T(8,128)(2,1)S(1)} %fusion.47), channel_id=1, source_target_pairs={{0,8},{8,16},{16,24},{24,0},{1,9},{9,17},{17,25},{25,1},{2,10},{10... | collective-permute-start | bytes 2752520 | tf_op jit(solution)/shard_map/ppermute | solution.py:30
  422.9 72.0 %all-to-all-start.5 = ((bf16[32,40,1792]{2,1,0:T(8,128)(2,1)}), bf16[32,40,1792]{2,1,0:T(8,128)(2,1)}, u32[]{:S(2)}, u32[]{:S(2)}) async-start(bf16[32,40,1792]{2,1,0:T(8,128)(2,1)} %bitcast.176), calls=%async_computation.5 | async-start | bytes 9175040 | tf_op jit(solution)/shard_map/all_to_all | solution.py:368
  (43 other events, 515.3 us)
